TPU v7x, 32 devices: a whole 2x2x4 slice. The times are simulated.
32 devices in a mesh: pole: 2 (over y), row: 4 (over x, core), col: 4 (over z).
Axes of the slice: x: 2, y: 2, z: 4, core: 2. Of those that a mesh axis runs over, the one named last changes fastest.
Arguments:
- inverse_blocks: float32 [4096, 2048], P(('pole', 'row'), 'col'), parts along dimension 0, may hold values from -6 to 6
- lower_panel: float32 [4096, 512], P(('pole', 'row'), 'col'), parts along dimension 0, may hold values from -0.125 to 0.125
- struct_mask: int32 [16, 4], P('row', 'col'), may hold values 0 or 1
- diag_inverse: float32 [1024, 128], P(('pole', 'col')), parts along dimension 0, may hold values from -6 to 6
Outputs:
- g_panel: float32 [4096, 512], P(('pole', 'row'), 'col'), parts along dimension 0
- g_diag: float32 [1024, 128], P(('pole', 'col')), parts along dimension 0
There are 2 independent parts, one for each index of `pole`. A program takes and returns all parts, laid end to end along the dimension named above; an argument that names none is the same for every part. Nothing has to cross between parts.
All inputs are finite; a program needn't handle non-finite values. No bound on the sum of `struct_mask` on one device may be relied on, other than what follows from the above.
Results may differ from a plain program's by a relative error of at most 0.000071.
Values sent between devices are 32-bit elements; how exact they have to be, the bound alone decides.
No kernel may reach another device: no remote copies, remote signals or barrier semaphores. Data moves between devices by JAX's collectives and lax.ppermute only.
A program may use at most 64 MiB of HBM per device.

v0:
```python
import jax
import jax.numpy as jnp
from jax import lax
from jax.sharding import PartitionSpec as P


def from_root(x, axis, root):
    mine = lax.axis_index(axis) == root
    return lax.psum(jnp.where(mine, x, jnp.zeros_like(x)), axis)


def on_device(inverse_blocks, lower_panel, struct_mask, diag_inverse):
    width = diag_inverse.shape[1]
    local_rows = lower_panel.shape[0]
    local_cols = lower_panel.shape[1]
    supers = local_cols // width
    expanded = jnp.repeat(jnp.repeat(struct_mask, width, axis=0), width, axis=1).astype(jnp.float32)
    masked = lower_panel * expanded
    panel_row = lax.all_gather(masked, "col", axis=1, tiled=True)
    mirrored = from_root(panel_row, "row", lax.axis_index("col"))
    summed = lax.psum_scatter(
        lax.dot_general(
            mirrored,
            inverse_blocks,
            (((0,), (1,)), ((), ())),
            precision=lax.Precision.HIGHEST,
            preferred_element_type=jnp.float32,
        ),
        "col",
        scatter_dimension=0,
        tiled=True,
    )
    g_panel = -summed.T * expanded
    masked_three = masked.reshape(local_rows, supers, width)
    panel_three = g_panel.reshape(local_rows, supers, width)
    quad_part = -jnp.einsum(
        "jka,jkb->kab", masked_three, panel_three, precision=lax.Precision.HIGHEST
    )
    quad_total = lax.psum(quad_part, "row")
    g_diag = diag_inverse + quad_total.reshape(supers * width, width)
    return (g_panel, g_diag)


def solution(mesh):
    placed = (
        P(("pole", "row"), "col"),
        P(("pole", "row"), "col"),
        P("row", "col"),
        P(("pole", "col"), None),
    )
    return jax.shard_map(
        on_device,
        mesh=mesh,
        in_specs=placed,
        out_specs=(P(("pole", "row"), "col"), P(("pole", "col"), None)),
        check_vma=False,
    )
```

profile of v0, /device:TPU:0, one launch (start us, length us, event | category | flops | bytes accessed | tf_op | source)
XLA Modules:
  0.0 153.8 jit_solution(16746672606810595600)
XLA Ops:
  7.2 0.0 copy-start
  7.2 0.0 all-gather.2.cloned.1.call-start
  7.2 0.7 convert_bitcast_fusion
  8.0 0.1 broadcast_bitcast_fusion
  8.0 1.8 %broadcast_multiply_fusion = f32[512,128]{1,0:T(8,128)} fusion(f32[512,128]{1,0:T(8,128)} %param.5, f32[512]{0:T(512)S(1)} %broadcast_bitcast_fusion), kind=kLoop, calls=%fused_computation.5 | loop fusion | flops 65536 | bytes 526336 | tf_op jit(solution)/shard_map/mul | solution.py:18
  9.8 0.0 all-gather.2.cloned.1.call-update
  9.8 0.0 all-reduce.3.cloned.1.call-start
  9.9 33.2 %all-gather.2.cloned.1.call-done = f32[512,512]{1,0:T(8,128)} async-done(((f32[512,128]{1,0:T(8,128)}), f32[512,512]{1,0:T(8,128)}) %all-gather.2.cloned.1.call-update) | async-done | bytes 1048592 | tf_op jit(solution)/shard_map/all_gather | solution.py:19
  43.1 2.3 %broadcast_select_fusion = f32[512,512]{1,0:T(8,128)} fusion(f32[512,512]{1,0:T(8,128)} %all-gather.2.cloned.1.call-done, pred[]{:T(512)S(6)} %eq.3), kind=kLoop, calls=%fused_computation.1 | loop fusion | flops 262144 | bytes 2097153 | tf_op jit(solution)/shard_map/jit(_where)/select_n | solution.py:9
  45.4 0.0 all-reduce.3.cloned.1.call-update
  45.4 0.0 reduce-scatter.2.cloned.1.call-start
  45.5 34.4 %all-reduce.3.cloned.1.call-done = f32[512,512]{1,0:T(8,128)} async-done(((f32[512,512]{1,0:T(8,128)}), f32[512,512]{1,0:T(8,128)}) %all-reduce.3.cloned.1.call-update) | async-done | bytes 1048592 | tf_op jit(solution)/shard_map/psum | solution.py:9
  79.9 0.0 copy-done
  79.9 5.7 %fusion.2 = f32[512,512]{1,0:T(8,128)} fusion(f32[512,512]{1,0:T(8,128)} %all-reduce.3.cloned.1.call-done, f32[512,512]{1,0:T(8,128)S(1)} %copy-done), kind=kOutput, calls=%fused_computation.8 | convolution fusion | flops 1610612736 | bytes 3145728 | tf_op jit(solution)/shard_map/dot_general | solution.py:22
  85.6 0.0 copy-start.1
  85.6 0.0 reduce-scatter.2.cloned.1.call-update
  85.7 0.0 all-reduce.5.cloned.1.call-start
  85.7 27.6 %reduce-scatter.2.cloned.1.call-done = f32[128,512]{1,0:T(8,128)} async-done(((f32[512,512]{1,0:T(8,128)}), f32[128,512]{1,0:T(8,128)}) %reduce-scatter.2.cloned.1.call-update) | async-done | bytes 262160 | tf_op jit(solution)/shard_map/reduce_scatter | solution.py:21
  113.3 0.0 copy-done.1
  113.4 0.0 copy-start.2
  113.4 2.3 %convolution_negate_fusion = f32[128,128]{1,0:T(8,128)} fusion(f32[128,512]{1,0:T(8,128)} %reduce-scatter.2.cloned.1.call-done, f32[512]{0:T(512)S(1)} %broadcast_bitcast_fusion, f32[512,128]{1,0:T(8,128)S(1)} %copy-done.1), kind=kOutput, calls=%fused_computation | convolution fusion | flops 100876288 | bytes 591872 | tf_op jit(solution)/shard_map/jka,jkb->kab/dot_general | solution.py:36
  115.7 0.0 all-reduce.5.cloned.1.call-update
  115.7 0.0 copy-done.2
  115.8 0.0 copy-start.3
  115.8 0.8 copy.6
  116.6 29.2 %all-reduce.5.cloned.1.call-done = f32[128,128]{1,0:T(8,128)} async-done(((f32[128,128]{1,0:T(8,128)}), f32[128,128]{1,0:T(8,128)}) %all-reduce.5.cloned.1.call-update) | async-done | bytes 65552 | tf_op jit(solution)/shard_map/psum | solution.py:39
  145.8 0.0 copy-done.3
  145.8 1.5 add.9
  (1 shorter events, 0.0 us)
Async XLA Ops:
  7.2 72.7 %copy-start = (f32[512,512]{1,0:T(8,128)S(1)}, f32[512,512]{1,0:T(8,128)}, u32[]{:S(2)}) copy-start(f32[512,512]{1,0:T(8,128)} %param.4) | copy-start | bytes 3145732
  7.2 35.9 %all-gather.2.cloned.1.call-start = ((), (), s32[]{:S(2)}) async-start(), calls=%async_computation.1 | async-start | bytes 1310720 | tf_op jit(solution)/shard_map/all_gather | solution.py:19
  9.8 70.1 %all-reduce.3.cloned.1.call-start = ((), (), s32[]{:S(2)}) async-start(), calls=%async_computation.2 | async-start | bytes 2097152 | tf_op jit(solution)/shard_map/psum | solution.py:9
  45.4 67.9 %reduce-scatter.2.cloned.1.call-start = ((), (), s32[]{:S(2)}) async-start(), calls=%async_computation.3 | async-start | bytes 1310720 | tf_op jit(solution)/shard_map/reduce_scatter | solution.py:21
  85.6 27.7 %copy-start.1 = (f32[512,128]{1,0:T(8,128)S(1)}, f32[512,128]{1,0:T(8,128)}, u32[]{:S(2)}) copy-start(f32[512,128]{1,0:T(8,128)} %param.5) | copy-start | bytes 786436
  85.7 60.2 %all-reduce.5.cloned.1.call-start = ((), (), s32[]{:S(2)}) async-start(), calls=%async_computation.4 | async-start | bytes 131072 | tf_op jit(solution)/shard_map/psum | solution.py:39
  113.4 2.4 %copy-start.2 = (f32[128,512]{1,0:T(8,128)S(1)}, f32[128,512]{1,0:T(8,128)}, u32[]{:S(2)}) copy-start(f32[128,512]{1,0:T(8,128)} %reduce-scatter.2.cloned.1.call-done) | copy-start | bytes 786436
  115.8 30.1 %copy-start.3 = (f32[128,128]{1,0:T(8,128)S(1)}, f32[128,128]{1,0:T(8,128)}, u32[]{:S(2)}) copy-start(f32[128,128]{1,0:T(8,128)} %param.7) | copy-start | bytes 196612
Sparse Core Ops, SparseCore 0:
  10.1 32.8 all-gather.1
  45.6 34.2 all-reduce.2
  85.8 27.5 reduce-scatter.1
  116.1 29.6 all-reduce.4
where the time goes:
time: 154 us
  waiting for transfers between devices  124 us (81%)
  between operations  13.8 us (9%)
  matrix products  8.07 us (5%)
  other arithmetic  6.37 us (4%)
    psum x1, waiting for transfers between devices, from_root(): return lax.psum(jnp.where(mine, x, jnp.zeros_like(x)), axis)  34.4 us
    all_gather x1, waiting for transfers between devices, on_device(): panel_row = lax.all_gather(masked, 'col', axis=1, tiled=True)  33.2 us
    psum x1, waiting for transfers between devices, on_device(): quad_total = lax.psum(quad_part, 'row')  29.2 us
    reduce_scatter x1, waiting for transfers between devices, on_device(): lax.psum_scatter(lax.dot_general(mirrored, inverse_blocks, (((0,), (1,)),...  27.6 us
    dot_general x1, matrix products, on_device(): lax.dot_general(mirrored, inverse_blocks, (((0,), (1,)), ((), ())), preci...  5.73 us
  transfers between devices with their start and end apart: 4, of which 4 were waited for; matrix products, arithmetic and copies ran while one was open for 1% of the time, Pallas kernels for 0%

commit v1 on v0

--- a/solution.py
+++ b/solution.py
@@ -2,6 +2,17 @@
 import jax.numpy as jnp
 from jax import lax
 from jax.sharding import PartitionSpec as P
+
+
+def turned_line(array, name, d):
+    size = lax.axis_size(name)
+    route = [(i, (i + 1) % size) for i in range(size)]
+    parts = [array]
+    for stride in range(1, size):
+        parts = [lax.ppermute(parts[0], name, route), *parts]
+    whole = jnp.concatenate(parts, axis=d)
+    shift = (lax.axis_index(name) + 1) * parts[-1].shape[d]
+    return jnp.roll(whole, shift, axis=d)
 
 
 def from_root(x, axis, root):
@@ -16,7 +27,7 @@
     supers = local_cols // width
     expanded = jnp.repeat(jnp.repeat(struct_mask, width, axis=0), width, axis=1).astype(jnp.float32)
     masked = lower_panel * expanded
-    panel_row = lax.all_gather(masked, "col", axis=1, tiled=True)
+    panel_row = turned_line(masked, "col", 1)
     mirrored = from_root(panel_row, "row", lax.axis_index("col"))
     summed = lax.psum_scatter(
         lax.dot_general(

time: 154 us -> 148 us (0.961)
  waiting for transfers between devices: 124 us -> 116 us
  starting transfers between devices: 0.16 us -> 3.2 us
    all_gather x1 -> x0, waiting for transfers between devices: 33.2 us -> none  [on_device(): panel_row = lax.all_gather(masked, 'col', axis=1, tiled=True)]
    ppermute x0 -> x3, waiting for transfers between devices: none -> 26 us  [turned_line(): parts = [lax.ppermute(parts[0], name, route), *parts]]
    ppermute x0 -> x3, starting transfers between devices: none -> 3.08 us  [turned_line(): parts = [lax.ppermute(parts[0], name, route), *parts]]
  transfers between devices with their start and end apart: 4 -> 6, of which waited for: 4 -> 6; matrix products, arithmetic and copies ran while one was open for 1% -> 1% of each run, Pallas kernels for 0% -> 0%
where the time goes in v1:
time: 148 us
  waiting for transfers between devices  116 us (78%)
  between operations  13.8 us (9%)
  matrix products  8.01 us (5%)
  other arithmetic  5.73 us (4%)
  starting transfers between devices  3.2 us (2%)
    psum x1, waiting for transfers between devices, from_root(): return lax.psum(jnp.where(mine, x, jnp.zeros_like(x)), axis)  34 us
    psum x1, waiting for transfers between devices, on_device(): quad_total = lax.psum(quad_part, 'row')  28.5 us
    reduce_scatter x1, waiting for transfers between devices, on_device(): lax.psum_scatter(lax.dot_general(mirrored, inverse_blocks, (((0,), (1,)),...  27.6 us
    ppermute x3, waiting for transfers between devices, turned_line(): parts = [lax.ppermute(parts[0], name, route), *parts]  26 us
    dot_general x1, matrix products, on_device(): lax.dot_general(mirrored, inverse_blocks, (((0,), (1,)), ((), ())), preci...  5.74 us
    ppermute x3, starting transfers between devices, turned_line(): parts = [lax.ppermute(parts[0], name, route), *parts]  3.08 us
  transfers between devices with their start and end apart: 6, of which 6 were waited for; matrix products, arithmetic and copies ran while one was open for 1% of the time, Pallas kernels for 0%

profile of v1, /device:TPU:0, one launch (start us, length us, event | category | flops | bytes accessed | tf_op | source)
XLA Modules:
  0.0 148.1 jit_solution(10218133313188352761)
XLA Ops:
  7.2 0.0 copy-start
  7.2 0.0 copy-start.1
  7.2 0.0 all-reduce.3.cloned.1.call-start
  7.2 0.8 convert_bitcast_fusion
  8.0 0.1 broadcast_bitcast_fusion
  8.1 1.1 broadcast_multiply_fusion
  9.2 3.1 %collective-permute-start = (f32[512,128]{1,0:T(8,128)S(1)}, f32[512,128]{1,0:T(8,128)S(1)}, u32[]{:S(2)}, u32[]{:S(2)}) collective-permute-start(f32[512,128]{1,0:T(8,128)S(1)} %broadcast_multiply_fusion), channel_id=1, source_target_pairs={{0,1},{1,2},{2,3},{3,0},{4,5},{5,6},{6,7},{7,4},{8,9},{9,10},{10,1... | collective-permute-start | bytes 786440 | tf_op jit(solution)/shard_map/ppermute | solution.py:12
  12.2 8.3 %collective-permute-done = f32[512,128]{1,0:T(8,128)S(1)} collective-permute-done((f32[512,128]{1,0:T(8,128)S(1)}, f32[512,128]{1,0:T(8,128)S(1)}, u32[]{:S(2)}, u32[]{:S(2)}) %collective-permute-start) | collective-permute-done | bytes 262176 | tf_op jit(solution)/shard_map/ppermute | solution.py:12
  20.6 0.0 collective-permute-start.1
  20.6 9.3 %collective-permute-done.1 = f32[512,128]{1,0:T(8,128)S(1)} collective-permute-done((f32[512,128]{1,0:T(8,128)S(1)}, f32[512,128]{1,0:T(8,128)S(1)}, u32[]{:S(2)}, u32[]{:S(2)}) %collective-permute-start.1) | collective-permute-done | bytes 262176 | tf_op jit(solution)/shard_map/ppermute | solution.py:12
  29.9 0.0 collective-permute-start.2
  29.9 8.4 %collective-permute-done.2 = f32[512,128]{1,0:T(8,128)S(1)} collective-permute-done((f32[512,128]{1,0:T(8,128)S(1)}, f32[512,128]{1,0:T(8,128)S(1)}, u32[]{:S(2)}, u32[]{:S(2)}) %collective-permute-start.2) | collective-permute-done | bytes 262176 | tf_op jit(solution)/shard_map/ppermute | solution.py:12
  38.3 0.0 copy-done.1
  38.3 0.1 constant_dynamic-update-slice_fusion.4
  38.6 0.1 constant_dynamic-update-slice_fusion
  38.7 1.2 dynamic-slice_select_fusion
  39.9 0.0 all-reduce.3.cloned.1.call-update
  39.9 0.0 reduce-scatter.2.cloned.1.call-start
  40.0 34.0 %all-reduce.3.cloned.1.call-done = f32[512,512]{1,0:T(8,128)} async-done(((f32[512,512]{1,0:T(8,128)}), f32[512,512]{1,0:T(8,128)}) %all-reduce.3.cloned.1.call-update) | async-done | bytes 1048592 | tf_op jit(solution)/shard_map/psum | solution.py:20
  74.0 0.0 copy-done
  74.0 5.7 %fusion.2 = f32[512,512]{1,0:T(8,128)} fusion(f32[512,512]{1,0:T(8,128)} %all-reduce.3.cloned.1.call-done, f32[512,512]{1,0:T(8,128)S(1)} %copy-done), kind=kOutput, calls=%fused_computation.16 | convolution fusion | flops 1610612736 | bytes 3145728 | tf_op jit(solution)/shard_map/dot_general | solution.py:33
  79.7 0.0 copy-start.2
  79.7 0.0 reduce-scatter.2.cloned.1.call-update
  79.7 0.0 all-reduce.5.cloned.1.call-start
  79.8 27.6 %reduce-scatter.2.cloned.1.call-done = f32[128,512]{1,0:T(8,128)} async-done(((f32[512,512]{1,0:T(8,128)}), f32[128,512]{1,0:T(8,128)}) %reduce-scatter.2.cloned.1.call-update) | async-done | bytes 262160 | tf_op jit(solution)/shard_map/reduce_scatter | solution.py:32
  107.4 2.3 %convolution_negate_fusion = f32[128,128]{1,0:T(8,128)} fusion(f32[128,512]{1,0:T(8,128)} %reduce-scatter.2.cloned.1.call-done, f32[512]{0:T(512)S(1)} %broadcast_bitcast_fusion, f32[512,128]{1,0:T(8,128)S(1)} %copy-done.1), kind=kOutput, calls=%fused_computation | convolution fusion | flops 100876288 | bytes 591872 | tf_op jit(solution)/shard_map/jka,jkb->kab/dot_general | solution.py:47
  109.7 0.0 all-reduce.5.cloned.1.call-update
  109.7 1.0 fusion
  110.7 0.8 copy.6
  111.5 28.5 %all-reduce.5.cloned.1.call-done = f32[128,128]{1,0:T(8,128)} async-done(((f32[128,128]{1,0:T(8,128)}), f32[128,128]{1,0:T(8,128)}) %all-reduce.5.cloned.1.call-update) | async-done | bytes 65552 | tf_op jit(solution)/shard_map/psum | solution.py:50
  140.0 0.0 copy-done.2
  140.0 1.5 add.25
  (6 shorter events, 0.2 us)
Async XLA Ops:
  7.2 66.8 %copy-start = (f32[512,512]{1,0:T(8,128)S(1)}, f32[512,512]{1,0:T(8,128)}, u32[]{:S(2)}) copy-start(f32[512,512]{1,0:T(8,128)} %param.4) | copy-start | bytes 3145732
  7.2 31.2 %copy-start.1 = (f32[512,128]{1,0:T(8,128)S(1)}, f32[512,128]{1,0:T(8,128)}, u32[]{:S(2)}) copy-start(f32[512,128]{1,0:T(8,128)} %param.5) | copy-start | bytes 786436
  7.2 66.8 %all-reduce.3.cloned.1.call-start = ((), (), s32[]{:S(2)}) async-start(), calls=%async_computation.1 | async-start | bytes 2097152 | tf_op jit(solution)/shard_map/psum | solution.py:20
  9.2 11.4 %collective-permute-start = (f32[512,128]{1,0:T(8,128)S(1)}, f32[512,128]{1,0:T(8,128)S(1)}, u32[]{:S(2)}, u32[]{:S(2)}) collective-permute-start(f32[512,128]{1,0:T(8,128)S(1)} %broadcast_multiply_fusion), channel_id=1, source_target_pairs={{0,1},{1,2},{2,3},{3,0},{4,5},{5,6},{6,7},{7,4},{8,9},{9,10},{10,1... | collective-permute-start | bytes 786440 | tf_op jit(solution)/shard_map/ppermute | solution.py:12
  20.6 9.3 %collective-permute-start.1 = (f32[512,128]{1,0:T(8,128)S(1)}, f32[512,128]{1,0:T(8,128)S(1)}, u32[]{:S(2)}, u32[]{:S(2)}) collective-permute-start(f32[512,128]{1,0:T(8,128)S(1)} %collective-permute-done), channel_id=1, source_target_pairs={{0,1},{1,2},{2,3},{3,0},{4,5},{5,6},{6,7},{7,4},{8,9},{9,10},{10,1... | collective-permute-start | bytes 786440 | tf_op jit(solution)/shard_map/ppermute | solution.py:12
  29.9 8.4 %collective-permute-start.2 = (f32[512,128]{1,0:T(8,128)S(1)}, f32[512,128]{1,0:T(8,128)S(1)}, u32[]{:S(2)}, u32[]{:S(2)}) collective-permute-start(f32[512,128]{1,0:T(8,128)S(1)} %collective-permute-done.1), channel_id=1, source_target_pairs={{0,1},{1,2},{2,3},{3,0},{4,5},{5,6},{6,7},{7,4},{8,9},{9,10},{10,1... | collective-permute-start | bytes 786440 | tf_op jit(solution)/shard_map/ppermute | solution.py:12
  39.9 67.5 %reduce-scatter.2.cloned.1.call-start = ((), (), s32[]{:S(2)}) async-start(), calls=%async_computation.2 | async-start | bytes 1310720 | tf_op jit(solution)/shard_map/reduce_scatter | solution.py:32
  79.7 60.3 %copy-start.2 = (f32[128,128]{1,0:T(8,128)S(1)}, f32[128,128]{1,0:T(8,128)}, u32[]{:S(2)}) copy-start(f32[128,128]{1,0:T(8,128)} %param.7) | copy-start | bytes 196612
  79.7 60.3 %all-reduce.5.cloned.1.call-start = ((), (), s32[]{:S(2)}) async-start(), calls=%async_computation.3 | async-start | bytes 131072 | tf_op jit(solution)/shard_map/psum | solution.py:50
Sparse Core Ops, SparseCore 0:
  40.0 33.8 all-reduce.2
  79.8 27.5 reduce-scatter.1
  110.3 29.6 all-reduce.4

commit v2 on v0

--- a/solution.py
+++ b/solution.py
@@ -36,7 +36,17 @@
     quad_part = -jnp.einsum(
         "jka,jkb->kab", masked_three, panel_three, precision=lax.Precision.HIGHEST
     )
-    quad_total = lax.psum(quad_part, "row")
+
+    def rails_bring(raw):
+        val2 = raw
+        n_slots = jax.lax.axis_size("row")
+        for i0 in [i for i in (1, 2, 4, 8, 16) if i < n_slots]:
+            val2 = val2 + jax.lax.ppermute(
+                val2, axis_name="row", perm=[(s, s ^ i0) for s in range(n_slots)]
+            )
+        return val2
+
+    quad_total = rails_bring(quad_part)
     g_diag = diag_inverse + quad_total.reshape(supers * width, width)
     return (g_panel, g_diag)
 

time: 154 us -> 128 us (0.83)
  waiting for transfers between devices: 124 us -> 98.5 us
  starting transfers between devices: 0.16 us -> 1.73 us
    psum x1 -> x0, waiting for transfers between devices: 29.2 us -> none  [on_device(): quad_total = lax.psum(quad_part, 'row')]
    ppermute x0 -> x2, waiting for transfers between devices: none -> 3.16 us  [rails_bring(): jax.lax.ppermute(val2, axis_name='row', perm=[(s, s ^ i0) for s in range(...]
    ppermute x0 -> x2, starting transfers between devices: none -> 1.61 us  [rails_bring(): jax.lax.ppermute(val2, axis_name='row', perm=[(s, s ^ i0) for s in range(...]
  transfers between devices with their start and end apart: 4 -> 5, of which waited for: 4 -> 5; matrix products, arithmetic and copies ran while one was open for 1% -> 1% of each run, Pallas kernels for 0% -> 0%
where the time goes in v2:
time: 128 us
  waiting for transfers between devices  98.5 us (77%)
  between operations  13.8 us (11%)
  matrix products  7.43 us (6%)
  other arithmetic  5.53 us (4%)
  starting transfers between devices  1.73 us (1%)
    psum x1, waiting for transfers between devices, from_root(): return lax.psum(jnp.where(mine, x, jnp.zeros_like(x)), axis)  34.4 us
    all_gather x1, waiting for transfers between devices, on_device(): panel_row = lax.all_gather(masked, 'col', axis=1, tiled=True)  33.2 us
    reduce_scatter x1, waiting for transfers between devices, on_device(): lax.psum_scatter(lax.dot_general(mirrored, inverse_blocks, (((0,), (1,)),...  27.7 us
    dot_general x1, matrix products, on_device(): lax.dot_general(mirrored, inverse_blocks, (((0,), (1,)), ((), ())), preci...  5.72 us
    ppermute x2, waiting for transfers between devices, rails_bring(): jax.lax.ppermute(val2, axis_name='row', perm=[(s, s ^ i0) for s in range(...  3.16 us
  transfers between devices with their start and end apart: 5, of which 5 were waited for; matrix products, arithmetic and copies ran while one was open for 1% of the time, Pallas kernels for 0%

profile of v2, /device:TPU:0, one launch (start us, length us, event | category | flops | bytes accessed | tf_op | source)
XLA Modules:
  0.0 127.9 jit_solution(2569486048996821685)
XLA Ops:
  7.2 0.0 copy-start
  7.2 0.0 all-gather.2.cloned.1.call-start
  7.2 0.7 convert_bitcast_fusion
  8.0 0.1 broadcast_bitcast_fusion
  8.0 1.8 %broadcast_multiply_fusion = f32[512,128]{1,0:T(8,128)} fusion(f32[512,128]{1,0:T(8,128)} %param.5, f32[512]{0:T(512)S(1)} %broadcast_bitcast_fusion), kind=kLoop, calls=%fused_computation.6 | loop fusion | flops 65536 | bytes 526336 | tf_op jit(solution)/shard_map/mul | solution.py:18
  9.8 0.0 all-gather.2.cloned.1.call-update
  9.8 0.0 all-reduce.2.cloned.1.call-start
  9.9 33.2 %all-gather.2.cloned.1.call-done = f32[512,512]{1,0:T(8,128)} async-done(((f32[512,128]{1,0:T(8,128)}), f32[512,512]{1,0:T(8,128)}) %all-gather.2.cloned.1.call-update) | async-done | bytes 1048592 | tf_op jit(solution)/shard_map/all_gather | solution.py:19
  43.1 2.3 %broadcast_select_fusion = f32[512,512]{1,0:T(8,128)} fusion(f32[512,512]{1,0:T(8,128)} %all-gather.2.cloned.1.call-done, pred[]{:T(512)S(6)} %eq.3), kind=kLoop, calls=%fused_computation.2 | loop fusion | flops 262144 | bytes 2097153 | tf_op jit(solution)/shard_map/jit(_where)/select_n | solution.py:9
  45.4 0.0 all-reduce.2.cloned.1.call-update
  45.4 0.0 reduce-scatter.2.cloned.1.call-start
  45.5 34.4 %all-reduce.2.cloned.1.call-done = f32[512,512]{1,0:T(8,128)} async-done(((f32[512,512]{1,0:T(8,128)}), f32[512,512]{1,0:T(8,128)}) %all-reduce.2.cloned.1.call-update) | async-done | bytes 1048592 | tf_op jit(solution)/shard_map/psum | solution.py:9
  79.9 0.0 copy-done
  79.9 5.7 %fusion.3 = f32[512,512]{1,0:T(8,128)} fusion(f32[512,512]{1,0:T(8,128)} %all-reduce.2.cloned.1.call-done, f32[512,512]{1,0:T(8,128)S(1)} %copy-done), kind=kOutput, calls=%fused_computation.10 | convolution fusion | flops 1610612736 | bytes 3145728 | tf_op jit(solution)/shard_map/dot_general | solution.py:22
  85.6 0.0 copy-start.1
  85.6 0.0 reduce-scatter.2.cloned.1.call-update
  85.6 27.7 %reduce-scatter.2.cloned.1.call-done = f32[128,512]{1,0:T(8,128)} async-done(((f32[512,512]{1,0:T(8,128)}), f32[128,512]{1,0:T(8,128)}) %reduce-scatter.2.cloned.1.call-update) | async-done | bytes 262160 | tf_op jit(solution)/shard_map/reduce_scatter | solution.py:21
  113.3 0.0 copy-done.1
  113.3 0.0 copy-start.2
  113.3 1.7 %fusion = f32[1,128,128]{2,1,0:T(8,128)S(1)} fusion(f32[128,512]{1,0:T(8,128)} %reduce-scatter.2.cloned.1.call-done, f32[512]{0:T(512)S(1)} %broadcast_bitcast_fusion, f32[512,128]{1,0:T(8,128)S(1)} %copy-done.1), kind=kOutput, calls=%fused_computation.1 | convolution fusion | flops 100876288 | bytes 591872 | tf_op jit(solution)/shard_map/jka,jkb->kab/dot_general | solution.py:36
  115.0 0.1 collective-permute-start
  115.1 1.2 collective-permute-done
  116.4 1.5 %collective-permute-start.1 = (f32[1,128,128]{2,1,0:T(8,128)S(1)}, f32[1,128,128]{2,1,0:T(8,128)S(1)}, u32[]{:S(2)}, u32[]{:S(2)}) collective-permute-start(f32[1,128,128]{2,1,0:T(8,128)S(1)} %add.13), channel_id=1, source_target_pairs={{0,8},{4,12},{8,0},{12,4},{1,9},{5,13},{9,1},{13,5},{2,10},{6,14},... | collective-permute-start | bytes 196616 | tf_op jit(solution)/shard_map/ppermute | solution.py:44
  117.9 0.0 copy-done.2
  117.9 0.0 copy-start.3
  117.9 0.8 copy.6
  118.8 1.9 %collective-permute-done.1 = f32[1,128,128]{2,1,0:T(8,128)S(1)} collective-permute-done((f32[1,128,128]{2,1,0:T(8,128)S(1)}, f32[1,128,128]{2,1,0:T(8,128)S(1)}, u32[]{:S(2)}, u32[]{:S(2)}) %collective-permute-start.1) | collective-permute-done | bytes 65568 | tf_op jit(solution)/shard_map/ppermute | solution.py:44
  120.7 0.0 copy-done.3
  120.7 0.6 bitcast_add_fusion
  (2 shorter events, 0.0 us)
Async XLA Ops:
  7.2 72.7 %copy-start = (f32[512,512]{1,0:T(8,128)S(1)}, f32[512,512]{1,0:T(8,128)}, u32[]{:S(2)}) copy-start(f32[512,512]{1,0:T(8,128)} %param.4) | copy-start | bytes 3145732
  7.2 35.9 %all-gather.2.cloned.1.call-start = ((), (), s32[]{:S(2)}) async-start(), calls=%async_computation.1 | async-start | bytes 1310720 | tf_op jit(solution)/shard_map/all_gather | solution.py:19
  9.8 70.0 %all-reduce.2.cloned.1.call-start = ((), (), s32[]{:S(2)}) async-start(), calls=%async_computation.2 | async-start | bytes 2097152 | tf_op jit(solution)/shard_map/psum | solution.py:9
  45.4 67.9 %reduce-scatter.2.cloned.1.call-start = ((), (), s32[]{:S(2)}) async-start(), calls=%async_computation.3 | async-start | bytes 1310720 | tf_op jit(solution)/shard_map/reduce_scatter | solution.py:21
  85.6 27.7 %copy-start.1 = (f32[512,128]{1,0:T(8,128)S(1)}, f32[512,128]{1,0:T(8,128)}, u32[]{:S(2)}) copy-start(f32[512,128]{1,0:T(8,128)} %param.5) | copy-start | bytes 786436
  113.3 4.6 %copy-start.2 = (f32[128,512]{1,0:T(8,128)S(1)}, f32[128,512]{1,0:T(8,128)}, u32[]{:S(2)}) copy-start(f32[128,512]{1,0:T(8,128)} %reduce-scatter.2.cloned.1.call-done) | copy-start | bytes 786436
  115.0 1.3 %collective-permute-start = (f32[1,128,128]{2,1,0:T(8,128)S(1)}, f32[1,128,128]{2,1,0:T(8,128)S(1)}, u32[]{:S(2)}, u32[]{:S(2)}) collective-permute-start(f32[1,128,128]{2,1,0:T(8,128)S(1)} %fusion), channel_id=1, source_target_pairs={{0,4},{4,0},{8,12},{12,8},{1,5},{5,1},{9,13},{13,9},{2,6},{6,2},{1... | collective-permute-start | bytes 196616 | tf_op jit(solution)/shard_map/ppermute | solution.py:44
  116.4 4.3 %collective-permute-start.1 = (f32[1,128,128]{2,1,0:T(8,128)S(1)}, f32[1,128,128]{2,1,0:T(8,128)S(1)}, u32[]{:S(2)}, u32[]{:S(2)}) collective-permute-start(f32[1,128,128]{2,1,0:T(8,128)S(1)} %add.13), channel_id=1, source_target_pairs={{0,8},{4,12},{8,0},{12,4},{1,9},{5,13},{9,1},{13,5},{2,10},{6,14},... | collective-permute-start | bytes 196616 | tf_op jit(solution)/shard_map/ppermute | solution.py:44
  117.9 2.8 %copy-start.3 = (f32[128,128]{1,0:T(8,128)S(1)}, f32[128,128]{1,0:T(8,128)}, u32[]{:S(2)}) copy-start(f32[128,128]{1,0:T(8,128)} %param.7) | copy-start | bytes 196612
Sparse Core Ops, SparseCore 0:
  10.1 32.8 all-gather.1
  45.6 34.2 all-reduce.1
  85.7 27.5 reduce-scatter.1
